TPU v7x, 32 devices: a whole 2x2x4 slice. The times are simulated.
32 devices in a mesh: samples: 4 (over y, x), channel: 4 (over z), spatial: 2 (over core).
Axes of the slice: x: 2, y: 2, z: 4, core: 2. Of those that a mesh axis runs over, the one named last changes fastest.
Arguments:
- features: bfloat16 [512, 4, 2, 1024], P('channel', 'samples', 'spatial'), may hold values from -6 to 6
- conv_one: bfloat16 [27, 512, 512], P(None, 'channel'), may hold values from -0.0625 to 0.0625
- conv_two: bfloat16 [27, 512, 512], P(None, 'channel'), may hold values from -0.0625 to 0.0625
- cotangent: bfloat16 [512, 4, 2, 1024], P('channel', 'samples', 'spatial'), may hold values from -6 to 6
Outputs:
- mixed_out: bfloat16 [512, 4, 2, 1024], P('channel', 'samples', 'spatial')
- input_grad: bfloat16 [512, 4, 2, 1024], P('channel', 'samples', 'spatial')
- grad_one: float32 [27, 512, 512], P(None, 'channel')
- grad_two: float32 [27, 512, 512], P(None, 'channel')
All inputs are finite; a program needn't handle non-finite values.
Results may differ from a plain program's by a relative error of at most 0.017.
Values may be sent and summed in bfloat16 or wider, within the bound.
A program may use at most 128 MiB of HBM per device.

v0:
```python
import jax
import jax.numpy as jnp
from jax import lax
from jax.sharding import PartitionSpec as P

SIDE = 32


def with_halo(shard, sides, width):
    for axis, dim in sides:
        size, length = (lax.axis_size(axis), shard.shape[dim])
        up = [(i, (i + 1) % size) for i in range(size - 1)]
        down = [(j, i) for i, j in up]
        last = lax.slice_in_dim(shard, length - width, length, axis=dim)
        first = lax.slice_in_dim(shard, 0, width, axis=dim)
        before = lax.ppermute(last, axis, up)
        after = lax.ppermute(first, axis, down)
        shard = jnp.concatenate([before, shard, after], axis=dim)
    return shard


def to_grid(values):
    return values.reshape(values.shape[0], values.shape[1], values.shape[2], SIDE, SIDE)


def to_flat(values):
    return values.reshape(values.shape[0], values.shape[1], values.shape[2], SIDE * SIDE)


def as_taps(kernel):
    return kernel.reshape(3, 3, 3, kernel.shape[1], kernel.shape[2])


def forward_conv(source, kernel, rhs_spec):
    return lax.conv_general_dilated(
        source,
        as_taps(kernel),
        (1, 1, 1),
        [(0, 0), (1, 1), (1, 1)],
        dimension_numbers=("CNDHW", rhs_spec, "CNDHW"),
        preferred_element_type=jnp.float32,
    )


def data_grad(source, kernel, rhs_spec):
    flipped = as_taps(kernel)[::-1, ::-1, ::-1]
    return lax.conv_general_dilated(
        source,
        flipped,
        (1, 1, 1),
        [(0, 0), (1, 1), (1, 1)],
        dimension_numbers=("CNDHW", rhs_spec, "CNDHW"),
        preferred_element_type=jnp.float32,
    )


def weight_grad(padded, upstream, out_spec):
    result = lax.conv_general_dilated(
        padded,
        upstream,
        (1, 1, 1),
        [(0, 0), (0, 0), (0, 0)],
        dimension_numbers=("NCDHW", "OIDHW", out_spec),
        preferred_element_type=jnp.float32,
    )
    return result.reshape(27, result.shape[3], result.shape[4])


def pad_plane(values):
    return jnp.pad(values, ((0, 0), (0, 0), (0, 0), (1, 1), (1, 1)))


def body(features, conv_one, conv_two, cotangent):
    rims_x = with_halo(features, (("spatial", 2),), 1)
    whole_x = lax.all_gather(rims_x, "channel", axis=0, tiled=True)
    pre_act = forward_conv(to_grid(whole_x), conv_one, "DHWOI")
    hidden = jax.nn.silu(pre_act).astype(jnp.bfloat16)
    rims_h = with_halo(to_flat(hidden), (("spatial", 2),), 1)
    grid_h = to_grid(rims_h)
    weight_part = conv_two
    mixed_out = lax.psum_scatter(
        to_flat(forward_conv(grid_h, weight_part, "DHWIO")),
        "channel",
        scatter_dimension=0,
        tiled=True,
    ).astype(jnp.bfloat16)
    rims_c = with_halo(cotangent, (("spatial", 2),), 1)
    whole_c = to_grid(lax.all_gather(rims_c, "channel", axis=0, tiled=True))
    hidden_grad = data_grad(whole_c, conv_two, "DHWOI")
    sigmoid_v = jax.nn.sigmoid(pre_act)
    act_grad = (hidden_grad * sigmoid_v * (1.0 + pre_act * (1.0 - sigmoid_v))).astype(jnp.bfloat16)
    rims_g = with_halo(to_flat(act_grad), (("spatial", 2),), 1)
    grid_g = to_grid(rims_g)
    weight_part = conv_one
    input_grad = lax.psum_scatter(
        to_flat(data_grad(grid_g, weight_part, "DHWIO")).astype(jnp.bfloat16),
        "channel",
        scatter_dimension=0,
        tiled=True,
    )
    local_two = weight_grad(pad_plane(grid_h), whole_c[:, :, 1:-1], "DHWNC")
    local_one = weight_grad(pad_plane(to_grid(whole_x)), act_grad, "DHWCN")
    grad_one, grad_two = (
        lax.psum(local_one.astype(jnp.bfloat16), ("samples", "spatial")).astype(jnp.float32),
        lax.psum(local_two.astype(jnp.bfloat16), ("samples", "spatial")).astype(jnp.float32),
    )
    return (mixed_out, input_grad, grad_one, grad_two)


def solution(mesh):
    placed = (
        P("channel", "samples", "spatial", None),
        P(None, "channel", None),
        P(None, "channel", None),
        P("channel", "samples", "spatial", None),
    )
    return jax.shard_map(
        body,
        mesh=mesh,
        in_specs=placed,
        out_specs=(
            P("channel", "samples", "spatial", None),
            P("channel", "samples", "spatial", None),
            P(None, "channel", None),
            P(None, "channel", None),
        ),
        check_vma=False,
    )
```

profile of v0, /device:TPU:0, one launch (start us, length us, event | category | flops | bytes accessed | tf_op | source)
XLA Modules:
  0.0 412.6 jit_solution(8968176364339753036)
XLA Ops:
  7.2 1.9 copy.91
  9.2 2.4 collective-permute-start
  11.6 1.3 collective-permute-start.1
  12.9 2.3 collective-permute-done.1
  15.2 1.9 pad_maximum_fusion.1
  17.2 1.8 copy.106
  19.0 2.0 collective-permute-start.4
  21.1 1.3 collective-permute-start.5
  22.4 2.3 collective-permute-done.5
  24.7 1.9 pad_maximum_fusion.2
  26.7 56.1 %all-gather.3.cloned.1.call-done = bf16[512,1,3,1024]{0,3,2,1:T(8,128)(2,1)} async-done(((bf16[128,1,3,1024]{0,3,2,1:T(8,128)(2,1)}), bf16[512,1,3,1024]{0,3,2,1:T(8,128)(2,1)}) %all-gather.3.cloned.1.call-update) | async-done | bytes 3145744 | tf_op jit(solution)/shard_map/all_gather | solution.py:75
  82.8 3.6 copy.144
  86.4 1.6 fusion.85
  88.0 2.2 copy.96
  90.7 10.3 %multiply_convert_fusion = (bf16[1,32,8,5,128]{4,2,3,1,0:T(8,128)(2,1)S(1)}, f32[1,32,8,5,128]{4,2,3,1,0:T(8,128)}) fusion(bf16[3,3,3,128,512]{4,3,2,1,0:T(8,128)(2,1)S(1)} %bitcast.81, bf16[512,3,32,1,7,2]{0,4,5,2,1,3:T(8,128)(2,1)S(1)} %slice.16, bf16[512,3,32,1,8,5]{0,4,5,2,1,3:T(8,128)(2,1)S(1)} %copy.96, pred[8,5]{0,1:T(8,128)(4,1)S(1)} %copy-done.15), kind=kOutput, calls=%fused_computation.63 | convolution fusion | flops 4452974592 | bytes 9830440 | tf_op jit(solution)/shard_map/conv_general_dilated | solution.py:35
  101.0 0.5 copy.153
  101.6 0.8 copy-done.6
  102.4 0.7 copy.136
  103.1 1.3 collective-permute-start.3
  104.4 4.6 %collective-permute-start.2 = (bf16[128,1,1,1024]{0,3,2,1:T(8,128)(2,1)}, bf16[128,1,1,1024]{0,3,2,1:T(8,128)(2,1)}, u32[]{:S(2)}, u32[]{:S(2)}) collective-permute-start(bf16[128,1,1,1024]{0,3,2,1:T(8,128)(2,1)} %bitcast.42), channel_id=1, source_target_pairs={{0,1},{2,3},{4,5},{6,7},{8,9},{10,11},{12,13},{14,15},{16,17},{18,... | collective-permute-start | bytes 786440 | tf_op jit(solution)/shard_map/ppermute | solution.py:16
  109.0 1.3 fusion.84
  110.3 3.5 fusion.83
  113.8 32.2 %all-gather.5.cloned.1.call-done = bf16[512,1,3,1024]{0,3,2,1:T(8,128)(2,1)} async-done(((bf16[128,1,3,1024]{0,3,2,1:T(8,128)(2,1)}), bf16[512,1,3,1024]{0,3,2,1:T(8,128)(2,1)}) %all-gather.5.cloned.1.call-update) | async-done | bytes 3145744 | tf_op jit(solution)/shard_map/all_gather | solution.py:88
  145.9 3.6 copy.147
  149.6 0.6 pad.8.clone
  150.2 2.2 copy.111
  152.4 0.4 slice.20
  152.9 9.7 %fusion.57 = bf16[1,32,8,5,128]{4,2,3,1,0:T(8,128)(2,1)S(1)} fusion(bf16[3,3,3,128,512]{4,3,2,1,0:T(8,128)(2,1)S(1)} %bitcast.105, bf16[512,3,32,1,7,2]{0,4,5,2,1,3:T(8,128)(2,1)S(1)} %slice.20, bf16[512,3,32,1,8,5]{0,4,5,2,1,3:T(8,128)(2,1)S(1)} %copy.111, f32[1,32,8,5,128]{4,2,3,1,0:T(8,128)S(1)} %copy-done.17, pred[8,5]{0,1:T(8,128)(4,1)S(1)} %copy-done.15), kind=kOutput, calls=%fused_computation.54 | convolution fusion | flops 4453629952 | bytes 9830440 | tf_op jit(solution)/shard_map/conv_general_dilated | solution.py:47
  162.7 0.8 copy.113
  163.5 2.1 collective-permute-start.6
  165.6 1.3 collective-permute-start.7
  166.9 1.8 copy.140
  168.7 1.8 copy.141
  170.5 0.4 copy.139
  170.9 0.4 copy.142
  171.3 2.2 copy.126
  173.6 1.5 fusion.25
  175.1 15.5 %fusion.32 = bf16[3,3,3,128,512,1]{3,4,2,5,1,0:T(8,128)(2,1)} fusion(bf16[512,3,32,8,5,1]{0,3,5,4,2,1:T(8,128)(2,1)S(1)} %get-tuple-element.26, bf16[512,3,32,8,5,1]{0,3,5,4,2,1:T(8,128)(2,1)S(1)} %copy.126, bf16[512,3,32,8,5,1]{0,3,5,4,2,1:T(8,128)(2,1)S(1)} %get-tuple-element.27, bf16[1,32,8,5,128]{4,2,3,1,0:T(8,128)(2,1)S(1)} %fusion.57, ...), kind=kOutput, calls=%fused_computation.36 | convolution fusion | flops 4472799232 | bytes 15663144 | tf_op jit(solution)/shard_map/conv_general_dilated | solution.py:58
  190.5 5.9 %copy.128 = bf16[27,128,512]{2,1,0:T(8,128)(2,1)} copy(bf16[27,128,512]{1,2,0:T(8,128)(2,1)} %bitcast.99) | data formatting | bytes 7077888 | tf_op jit(solution)/shard_map/convert_element_type | solution.py:104
  196.4 2.4 slice.28
  198.8 2.3 copy.100
  201.1 2.3 copy.99
  203.4 1.1 copy.114
  204.5 1.1 copy.115
  205.8 0.4 copy.117
  206.3 4.9 %select_convert_fusion = bf16[1,32,8,5,512]{4,2,3,1,0:T(8,128)(2,1)S(1)} fusion(bf16[3,3,3,128,512]{4,3,2,1,0:T(8,128)(2,1)S(1)} %bitcast.82, bf16[128,3,32,1,7,2]{0,4,5,2,1,3:T(8,128)(2,1)S(1)} %slice.22, bf16[128,3,32,1,8,5]{0,4,5,2,1,3:T(8,128)(2,1)S(1)} %copy.117, pred[8,5]{0,1:T(8,128)(4,1)S(1)} %copy-done.15), kind=kOutput, calls=%fused_computation.34 | convolution fusion | flops 4440915968 | bytes 6176808 | tf_op jit(solution)/shard_map/conv_general_dilated | solution.py:47
  211.2 0.4 copy.118
  211.7 0.6 copy.119
  212.3 1.3 copy.134
  213.7 4.4 %pad_maximum_fusion = bf16[128,1,3,32,32]{0,1,4,3,2:T(2,128)(2,1)S(1)} fusion(bf16[128,1,1,32,32]{0,1,4,3,2:T(2,128)(2,1)} %copy.100, bf16[128,1,1,32,32]{0,1,4,3,2:T(2,128)(2,1)S(1)} %bitcast.93, bf16[128,1,1,32,32]{0,1,4,3,2:T(2,128)(2,1)} %copy.99), kind=kLoop, calls=%fused_computation.40 | loop fusion | flops 786432 | bytes 1572864 | tf_op jit(solution)/shard_map/concatenate | solution.py:18
  218.1 20.5 %convolution_convert_fusion = bf16[3,3,3,128,512]{4,3,2,1,0:T(8,128)(2,1)} fusion(bf16[128,1,3,32,32]{0,1,4,3,2:T(2,128)(2,1)S(1)} %pad_maximum_fusion, bf16[512,1,1,32,32]{0,4,3,2,1:T(8,128)(2,1)} %slice.28), kind=kOutput, calls=%fused_computation.35 | convolution fusion | flops 3476226048 | bytes 5373952 | tf_op jit(solution)/shard_map/conv_general_dilated | solution.py:58
  239.3 0.4 copy.103
  239.8 1.1 copy-done.14
  240.9 5.0 %convolution_select_fusion = f32[1,32,8,5,512]{4,2,3,1,0:T(8,128)S(1)} fusion(bf16[3,3,3,128,512]{4,3,2,1,0:T(8,128)(2,1)S(1)} %bitcast.106, bf16[128,3,32,1,7,2]{0,4,5,2,1,3:T(8,128)(2,1)S(1)} %slice.18, bf16[128,3,32,1,8,5]{0,4,5,2,1,3:T(8,128)(2,1)S(1)} %copy.103, pred[8,5]{0,1:T(8,128)(4,1)S(1)} %copy-done.16), kind=kOutput, calls=%fused_computation.39 | convolution fusion | flops 4440260608 | bytes 7487528 | tf_op jit(solution)/shard_map/conv_general_dilated | solution.py:35
  245.9 1.5 copy.104
  247.6 2.6 copy.105
  250.3 1.1 copy.135
  251.4 0.9 copy.131
  252.2 103.9 %all-reduce.3.cloned.1.call-done = (bf16[27,128,512]{2,1,0:T(8,128)(2,1)}, bf16[27,128,512]{2,1,0:T(8,128)(2,1)}) async-done(((bf16[27,128,512]{2,1,0:T(8,128)(2,1)}, bf16[27,128,512]{2,1,0:T(8,128)(2,1)}), (bf16[27,128,512]{2,1,0:T(8,128)(2,1)}, bf16[27,128,512]{2,1,0:T(8,128)(2,1)})) %all-reduce.3.cloned.1.call-update) | async-done | bytes 7077904 | tf_op jit(solution)/shard_map/psum | solution.py:104
  356.2 6.1 %convert_element_type.52 = f32[27,128,512]{2,1,0:T(8,128)} convert(bf16[27,128,512]{2,1,0:T(8,128)(2,1)} %get-tuple-element.16) | non-fusion elementwise | flops 1769472 | bytes 10616832 | tf_op jit(solution)/shard_map/convert_element_type | solution.py:104
  362.2 4.0 convert_element_type.55
  366.2 35.9 %reduce-scatter.5.cloned.1.call-done = f32[128,1,1,1024]{0,3,2,1:T(8,128)} async-done(((f32[512,1,1,1024]{0,3,2,1:T(8,128)}), f32[128,1,1,1024]{0,3,2,1:T(8,128)}) %reduce-scatter.5.cloned.1.call-update) | async-done | bytes 524304 | tf_op jit(solution)/shard_map/reduce_scatter | solution.py:81
  402.1 1.8 convert_element_type.46
  403.8 1.8 copy.130
  (65 shorter events, 2.2 us)
Async XLA Ops:
  7.2 83.5 %copy-start = (bf16[27,128,512]{2,1,0:T(8,128)(2,1)S(1)}, bf16[27,128,512]{2,1,0:T(8,128)(2,1)}, u32[]{:S(2)}) copy-start(bf16[27,128,512]{2,1,0:T(8,128)(2,1)} %param.5) | copy-start | bytes 10616836
  7.2 75.6 %all-gather.3.cloned.1.call-start = ((), (), s32[]{:S(2)}) async-start(), calls=%async_computation.2 | async-start | bytes 3932160 | tf_op jit(solution)/shard_map/all_gather | solution.py:75
  9.2 3.7 collective-permute-start
  11.6 3.6 collective-permute-start.1
  17.2 128.8 %all-gather.5.cloned.1.call-start = ((), (), s32[]{:S(2)}) async-start(), calls=%async_computation.4 | async-start | bytes 3932160 | tf_op jit(solution)/shard_map/all_gather | solution.py:88
  19.0 3.4 collective-permute-start.4
  21.1 3.6 collective-permute-start.5
  26.6 223.6 %reduce-scatter.7.cloned.1.call-start = ((), (), s32[]{:S(2)}) async-start(), calls=%async_computation.5 | async-start | bytes 1310720
  88.0 22.3 %copy-start.2 = (bf16[512,3,32,1,40]{0,2,4,1,3:T(8,128)(2,1)}, bf16[512,3,32,1,40]{0,2,4,1,3:T(8,128)(2,1)S(1)}, u32[]{:S(2)}) copy-start(bf16[512,3,32,1,40]{0,2,4,1,3:T(8,128)(2,1)S(1)} %get-tuple-element.22) | copy-start | bytes 11796484
  88.0 2.7 copy-start.15
  101.6 0.8 copy-start.6
  103.1 95.7 %collective-permute-start.3 = (bf16[128,1,1,1024]{0,3,2,1:T(8,128)(2,1)}, bf16[128,1,1,1024]{0,3,2,1:T(8,128)(2,1)}, u32[]{:S(2)}, u32[]{:S(2)}) collective-permute-start(bf16[128,1,1,1024]{0,3,2,1:T(8,128)(2,1)} %bitcast.42), channel_id=1, source_target_pairs={{1,0},{3,2},{5,4},{7,6},{9,8},{11,10},{13,12},{15,14},{17,16},{19,... | collective-permute-start | bytes 786440 | tf_op jit(solution)/shard_map/ppermute | solution.py:17
  104.4 96.7 %collective-permute-start.2 = (bf16[128,1,1,1024]{0,3,2,1:T(8,128)(2,1)}, bf16[128,1,1,1024]{0,3,2,1:T(8,128)(2,1)}, u32[]{:S(2)}, u32[]{:S(2)}) collective-permute-start(bf16[128,1,1,1024]{0,3,2,1:T(8,128)(2,1)} %bitcast.42), channel_id=1, source_target_pairs={{0,1},{2,3},{4,5},{6,7},{8,9},{10,11},{12,13},{14,15},{16,17},{18,... | collective-permute-start | bytes 786440 | tf_op jit(solution)/shard_map/ppermute | solution.py:16
  150.2 2.7 copy-start.13
  150.2 2.7 copy-start.17
  152.9 14.1 %copy-start.5 = (bf16[512,3,32,1,8,4]{0,2,5,4,1,3:T(8,128)(2,1)S(1)}, bf16[512,3,32,1,8,4]{0,2,5,4,1,3:T(8,128)(2,1)}, u32[]{:S(2)}) copy-start(bf16[512,3,32,1,8,4]{0,2,5,4,1,3:T(8,128)(2,1)} %get-tuple-element.18) | copy-start | bytes 9437188
  162.7 4.3 %copy-start.11 = (bf16[128,1,1,32,32]{0,3,4,1,2:T(8,128)(2,1)}, bf16[128,1,1,32,32]{0,3,4,1,2:T(8,128)(2,1)S(1)}, u32[]{:S(2)}) copy-start(bf16[128,1,1,32,32]{0,3,4,1,2:T(8,128)(2,1)S(1)} %slice_bitcast_fusion.2) | copy-start | bytes 786436
  162.7 6.0 %copy-start.4 = (bf16[512,3,32,1,8,4]{0,2,5,4,1,3:T(8,128)(2,1)S(1)}, bf16[512,3,32,1,8,4]{0,2,5,4,1,3:T(8,128)(2,1)}, u32[]{:S(2)}) copy-start(bf16[512,3,32,1,8,4]{0,2,5,4,1,3:T(8,128)(2,1)} %get-tuple-element.19) | copy-start | bytes 9437188
  163.5 40.0 %collective-permute-start.6 = (bf16[128,1,1,1024]{0,3,2,1:T(8,128)(2,1)}, bf16[128,1,1,1024]{0,3,2,1:T(8,128)(2,1)}, u32[]{:S(2)}, u32[]{:S(2)}) collective-permute-start(bf16[128,1,1,1024]{0,3,2,1:T(8,128)(2,1)} %bitcast.20), channel_id=1, source_target_pairs={{0,1},{2,3},{4,5},{6,7},{8,9},{10,11},{12,13},{14,15},{16,17},{18,... | collective-permute-start | bytes 786440 | tf_op jit(solution)/shard_map/ppermute | solution.py:16
  165.6 38.9 %collective-permute-start.7 = (bf16[128,1,1,1024]{0,3,2,1:T(8,128)(2,1)}, bf16[128,1,1,1024]{0,3,2,1:T(8,128)(2,1)}, u32[]{:S(2)}, u32[]{:S(2)}) collective-permute-start(bf16[128,1,1,1024]{0,3,2,1:T(8,128)(2,1)} %bitcast.20), channel_id=1, source_target_pairs={{1,0},{3,2},{5,4},{7,6},{9,8},{11,10},{13,12},{15,14},{17,16},{19,... | collective-permute-start | bytes 786440 | tf_op jit(solution)/shard_map/ppermute | solution.py:17
  168.7 1.8 copy-start.10
  168.7 2.2 copy-start.9
  168.7 2.6 copy-start.3
  196.4 9.2 %copy-start.12 = (bf16[128,1,1,32,32]{0,3,4,1,2:T(8,128)(2,1)S(1)}, bf16[128,1,1,32,32]{0,3,4,1,2:T(8,128)(2,1)}, u32[]{:S(2)}) copy-start(bf16[128,1,1,32,32]{0,3,4,1,2:T(8,128)(2,1)} %copy-done.11) | copy-start | bytes 786436
  211.6 2.1 copy-start.7
  213.7 142.5 %all-reduce.3.cloned.1.call-start = ((), (), s32[]{:S(2)}) async-start(), calls=%async_computation.6 | async-start | bytes 14155776 | tf_op jit(solution)/shard_map/psum | solution.py:104
  238.7 163.4 %reduce-scatter.5.cloned.1.call-start = ((), (), s32[]{:S(2)}) async-start(), calls=%async_computation.3 | async-start | bytes 2621440 | tf_op jit(solution)/shard_map/reduce_scatter | solution.py:81
  238.9 2.0 copy-start.14
  238.9 2.0 copy-start.16
  356.2 6.1 %copy-start.8 = (bf16[27,128,512]{2,1,0:T(8,128)(2,1)S(1)}, bf16[27,128,512]{2,1,0:T(8,128)(2,1)}, u32[]{:S(2)}) copy-start(bf16[27,128,512]{2,1,0:T(8,128)(2,1)} %get-tuple-element.17) | copy-start | bytes 10616836
  362.2 43.4 %copy-start.1 = (bf16[27,128,512]{2,1,0:T(8,128)(2,1)S(1)}, bf16[27,128,512]{2,1,0:T(8,128)(2,1)}, u32[]{:S(2)}) copy-start(bf16[27,128,512]{2,1,0:T(8,128)(2,1)} %param.5) | copy-start | bytes 10616836
Sparse Core Ops, SparseCore 0:
  17.3 65.4 all-gather.2
  84.3 61.5 all-gather.4
  213.8 27.3 reduce-scatter.6
  245.0 111.0 all-reduce.2
  358.3 43.7 reduce-scatter.4
where the time goes:
time: 416 us; the launch traced here: 413 us
  waiting for transfers between devices  233 us (56%)
  matrix products  65.8 us (16%)
  local copies, waits for them, and re-layouts  61.1 us (15%)
  other arithmetic  21.6 us (5%)
  starting transfers between devices  16.5 us (4%)
  between operations  14.8 us (4%)
    psum x1, waiting for transfers between devices, body(): lax.psum(local_one.astype(jnp.bfloat16), ('samples', 'spatial'))  104 us
    all_gather x1, waiting for transfers between devices, body(): whole_x = lax.all_gather(rims_x, 'channel', axis=0, tiled=True)  56.1 us
    conv_general_dilated x2, matrix products, weight_grad(): lax.conv_general_dilated(padded, upstream, (1, 1, 1), [(0, 0), (0, 0), (0...  36 us
    reduce_scatter x1, waiting for transfers between devices, body(): lax.psum_scatter(to_flat(forward_conv(grid_h, weight_part, 'DHWIO')), 'ch...  35.9 us
    all_gather x1, waiting for transfers between devices, body(): whole_c = to_grid(lax.all_gather(rims_c, 'channel', axis=0, tiled=True))  32.2 us
    unnamed x52, local copies, waits for them, and re-layouts  24.2 us
    conv_general_dilated x2, matrix products, forward_conv(): lax.conv_general_dilated(source, as_taps(kernel), (1, 1, 1), [(0, 0), (1,...  15.2 us
    conv_general_dilated x2, matrix products, data_grad(): lax.conv_general_dilated(source, flipped, (1, 1, 1), [(0, 0), (1, 1), (1,...  14.6 us
  transfers between devices with their start and end apart: 13, of which 6 were waited for; matrix products, arithmetic and copies ran while one was open for 32% of the time, Pallas kernels for 0%

commit v1 on v0

--- a/solution.py
+++ b/solution.py
@@ -101,7 +101,9 @@
     local_two = weight_grad(pad_plane(grid_h), whole_c[:, :, 1:-1], "DHWNC")
     local_one = weight_grad(pad_plane(to_grid(whole_x)), act_grad, "DHWCN")
     grad_one, grad_two = (
-        lax.psum(local_one.astype(jnp.bfloat16), ("samples", "spatial")).astype(jnp.float32),
+        lax.psum(lax.psum(local_one.astype(jnp.bfloat16), "spatial"), "samples").astype(
+            jnp.float32
+        ),
         lax.psum(local_two.astype(jnp.bfloat16), ("samples", "spatial")).astype(jnp.float32),
     )
     return (mixed_out, input_grad, grad_one, grad_two)

time: 416 us -> 483 us (1.16)
  waiting for transfers between devices: 233 us -> 295 us
    psum x1 -> x3, waiting for transfers between devices: 104 us -> 135 us  [the longest x1 92.4 us: body(): lax.psum(lax.psum(local_one.astype(jnp.bfloat16), 'spatial'), 'samples')]
    unnamed x6 -> x8, waiting for transfers between devices: 0.1 us -> 24.4 us
    unnamed x52 -> x48, local copies, waits for them, and re-layouts: 24.2 us -> 29.6 us
    reduce_scatter x1, waiting for transfers between devices: 35.9 us -> 40.7 us  [body(): lax.psum_scatter(to_flat(forward_conv(grid_h, weight_part, 'DHWIO')), 'ch...]
  transfers between devices with their start and end apart: 13 -> 15, of which waited for: 6 -> 9; matrix products, arithmetic and copies ran while one was open for 32% -> 29% of each run, Pallas kernels for 0% -> 0%
where the time goes in v1:
time: 483 us; the launch traced here: 479 us
  waiting for transfers between devices  295 us (61%)
  matrix products  65.8 us (14%)
  local copies, waits for them, and re-layouts  64.1 us (13%)
  other arithmetic  22.1 us (5%)
  starting transfers between devices  16.4 us (3%)
  between operations  15.2 us (3%)
    psum x1, waiting for transfers between devices, body(): lax.psum(lax.psum(local_one.astype(jnp.bfloat16), 'spatial'), 'samples')  92.4 us
    all_gather x1, waiting for transfers between devices, body(): whole_x = lax.all_gather(rims_x, 'channel', axis=0, tiled=True)  56.1 us
    psum x1, waiting for transfers between devices, body(): lax.psum(local_two.astype(jnp.bfloat16), ('samples', 'spatial'))  42.8 us
    reduce_scatter x1, waiting for transfers between devices, body(): lax.psum_scatter(to_flat(forward_conv(grid_h, weight_part, 'DHWIO')), 'ch...  40.7 us
    conv_general_dilated x2, matrix products, weight_grad(): lax.conv_general_dilated(padded, upstream, (1, 1, 1), [(0, 0), (0, 0), (0...  35.6 us
    all_gather x1, waiting for transfers between devices, body(): whole_c = to_grid(lax.all_gather(rims_c, 'channel', axis=0, tiled=True))  32.5 us
    unnamed x48, local copies, waits for them, and re-layouts  29.6 us
    unnamed x8, waiting for transfers between devices  24.4 us
  transfers between devices with their start and end apart: 15, of which 9 were waited for; matrix products, arithmetic and copies ran while one was open for 29% of the time, Pallas kernels for 0%

profile of v1, /device:TPU:0, one launch (start us, length us, event | category | flops | bytes accessed | tf_op | source)
XLA Modules:
  0.0 478.9 jit_solution(12588483803326334955)
XLA Ops:
  7.2 1.9 copy.91
  9.2 2.4 collective-permute-start
  11.6 1.3 collective-permute-start.1
  12.9 2.3 collective-permute-done.1
  15.2 1.9 pad_maximum_fusion.1
  17.2 1.8 copy.106
  19.0 2.0 collective-permute-start.4
  21.0 1.3 collective-permute-start.5
  22.4 2.3 collective-permute-done.5
  24.7 1.9 pad_maximum_fusion.2
  26.7 56.1 %all-gather.3.cloned.1.call-done = bf16[512,1,3,1024]{0,3,2,1:T(8,128)(2,1)} async-done(((bf16[128,1,3,1024]{0,3,2,1:T(8,128)(2,1)}), bf16[512,1,3,1024]{0,3,2,1:T(8,128)(2,1)}) %all-gather.3.cloned.1.call-update) | async-done | bytes 3145744 | tf_op jit(solution)/shard_map/all_gather | solution.py:75
  82.8 3.6 copy.144
  86.4 1.3 fusion.85
  87.8 2.2 copy.96
  90.4 10.2 %multiply_convert_fusion = (bf16[1,32,8,5,128]{4,2,3,1,0:T(8,128)(2,1)S(1)}, f32[1,32,8,5,128]{4,2,3,1,0:T(8,128)}) fusion(bf16[3,3,3,128,512]{4,3,2,1,0:T(8,128)(2,1)S(1)} %bitcast.81, bf16[512,3,32,1,7,2]{0,4,5,2,1,3:T(8,128)(2,1)S(1)} %slice.16, bf16[512,3,32,1,8,5]{0,4,5,2,1,3:T(8,128)(2,1)S(1)} %copy.96, pred[8,5]{0,1:T(8,128)(4,1)S(1)} %copy-done.13), kind=kOutput, calls=%fused_computation.63 | convolution fusion | flops 4452974592 | bytes 9830440 | tf_op jit(solution)/shard_map/conv_general_dilated | solution.py:35
  100.7 0.5 copy.153
  101.3 0.8 copy-done.6
  102.1 0.7 copy.136
  102.8 1.3 collective-permute-start.3
  104.1 4.7 collective-permute-start.2
  108.8 1.3 fusion.84
  110.0 3.4 fusion.83
  113.5 32.5 %all-gather.5.cloned.1.call-done = bf16[512,1,3,1024]{0,3,2,1:T(8,128)(2,1)} async-done(((bf16[128,1,3,1024]{0,3,2,1:T(8,128)(2,1)}), bf16[512,1,3,1024]{0,3,2,1:T(8,128)(2,1)}) %all-gather.5.cloned.1.call-update) | async-done | bytes 3145744 | tf_op jit(solution)/shard_map/all_gather | solution.py:88
  145.9 3.6 copy.147
  149.6 0.6 pad.8.clone
  150.1 2.2 copy.111
  152.4 0.4 slice.20
  152.8 1.5 copy-done.4
  154.3 1.8 copy.140
  156.1 1.8 copy.141
  158.7 2.7 copy.126
  161.4 10.1 %fusion.57 = bf16[1,32,8,5,128]{4,2,3,1,0:T(8,128)(2,1)} fusion(bf16[3,3,3,128,512]{4,3,2,1,0:T(8,128)(2,1)S(1)} %bitcast.109, bf16[512,3,32,1,7,2]{0,4,5,2,1,3:T(8,128)(2,1)S(1)} %slice.20, bf16[512,3,32,1,8,5]{0,4,5,2,1,3:T(8,128)(2,1)S(1)} %copy.111, f32[1,32,8,5,128]{4,2,3,1,0:T(8,128)S(1)} %copy-done.15, pred[8,5]{0,1:T(8,128)(4,1)S(1)} %copy-done.13), kind=kOutput, calls=%fused_computation.54 | convolution fusion | flops 4453629952 | bytes 9830440 | tf_op jit(solution)/shard_map/conv_general_dilated | solution.py:47
  171.6 1.2 fusion.25
  172.8 15.5 %fusion.32 = bf16[3,3,3,128,512,1]{3,4,2,5,1,0:T(8,128)(2,1)} fusion(bf16[512,3,32,8,5,1]{0,3,5,4,2,1:T(8,128)(2,1)S(1)} %get-tuple-element.24, bf16[512,3,32,8,5,1]{0,3,5,4,2,1:T(8,128)(2,1)S(1)} %copy.126, bf16[512,3,32,8,5,1]{0,3,5,4,2,1:T(8,128)(2,1)S(1)} %get-tuple-element.25, bf16[1,32,8,5,128]{4,2,3,1,0:T(8,128)(2,1)S(1)} %copy-done.10, ...), kind=kOutput, calls=%fused_computation.36 | convolution fusion | flops 4472799232 | bytes 15663144 | tf_op jit(solution)/shard_map/conv_general_dilated | solution.py:58
  188.3 0.8 copy.112
  189.1 5.7 %copy.128 = bf16[27,128,512]{2,1,0:T(8,128)(2,1)} copy(bf16[27,128,512]{1,2,0:T(8,128)(2,1)} %bitcast.99) | data formatting | bytes 7077888 | tf_op jit(solution)/shard_map/convert_element_type | solution.py:104
  194.9 1.4 slice.28
  196.3 1.5 copy.100
  197.9 1.5 copy.99
  199.4 3.4 pad_maximum_fusion
  202.8 20.1 %convolution_convert_fusion = bf16[3,3,3,128,512]{4,3,2,1,0:T(8,128)(2,1)} fusion(bf16[128,1,3,32,32]{0,1,4,3,2:T(2,128)(2,1)S(1)} %pad_maximum_fusion, bf16[512,1,1,32,32]{0,4,3,2,1:T(8,128)(2,1)S(1)} %slice.28), kind=kOutput, calls=%fused_computation.35 | convolution fusion | flops 3476226048 | bytes 5373952 | tf_op jit(solution)/shard_map/conv_general_dilated | solution.py:58
  222.9 1.0 slice_bitcast_fusion.2
  224.0 1.3 collective-permute-start.6
  225.3 1.5 collective-permute-start.7
  227.0 1.8 collective-permute-done.7
  229.7 4.9 %select_convert_fusion = bf16[1,32,8,5,512]{4,2,3,1,0:T(8,128)(2,1)S(1)} fusion(bf16[3,3,3,128,512]{4,3,2,1,0:T(8,128)(2,1)S(1)} %bitcast.82, bf16[128,3,32,1,7,2]{0,4,5,2,1,3:T(8,128)(2,1)S(1)} %slice.22, bf16[128,3,32,1,8,5]{0,4,5,2,1,3:T(8,128)(2,1)S(1)} %copy.117, pred[8,5]{0,1:T(8,128)(4,1)S(1)} %copy-done.14), kind=kOutput, calls=%fused_computation.34 | convolution fusion | flops 4440915968 | bytes 6176808 | tf_op jit(solution)/shard_map/conv_general_dilated | solution.py:47
  235.1 1.5 copy.119
  236.6 2.3 copy.134
  239.3 1.6 copy.152
  241.8 1.1 copy-done.12
  242.9 4.9 %convolution_select_fusion = f32[1,32,8,5,512]{4,2,3,1,0:T(8,128)S(1)} fusion(bf16[3,3,3,128,512]{4,3,2,1,0:T(8,128)(2,1)S(1)} %bitcast.110, bf16[128,3,32,1,7,2]{0,4,5,2,1,3:T(8,128)(2,1)S(1)} %slice.18, bf16[128,3,32,1,8,5]{0,4,5,2,1,3:T(8,128)(2,1)S(1)} %copy.103, pred[8,5]{0,1:T(8,128)(4,1)S(1)} %copy-done.14), kind=kOutput, calls=%fused_computation.39 | convolution fusion | flops 4440260608 | bytes 7487528 | tf_op jit(solution)/shard_map/conv_general_dilated | solution.py:35
  247.9 1.5 copy.104
  249.7 2.6 copy.105
  252.4 0.7 all-reduce.6.cloned.1.call-update
  253.1 42.8 %all-reduce.8.cloned.1.call-done = bf16[27,128,512]{2,1,0:T(8,128)(2,1)} async-done(((bf16[27,128,512]{2,1,0:T(8,128)(2,1)}), bf16[27,128,512]{2,1,0:T(8,128)(2,1)}) %all-reduce.8.cloned.1.call-update) | async-done | bytes 3538960 | tf_op jit(solution)/shard_map/psum | solution.py:107
  295.9 5.9 %convert_element_type.55 = f32[27,128,512]{2,1,0:T(8,128)} convert(bf16[27,128,512]{2,1,0:T(8,128)(2,1)} %all-reduce.8.cloned.1.call-done) | non-fusion elementwise | flops 1769472 | bytes 10616832 | tf_op jit(solution)/shard_map/convert_element_type | solution.py:107
  301.8 23.6 %reduce-scatter.7.cloned.1.call-done = bf16[128,1024]{1,0:T(8,128)(2,1)} async-done(((bf16[512,1024]{1,0:T(8,128)(2,1)}), bf16[128,1024]{1,0:T(8,128)(2,1)}) %reduce-scatter.7.cloned.1.call-update) | async-done | bytes 262160
  325.4 1.8 copy.135
  327.2 1.8 copy.131
  329.0 40.7 %reduce-scatter.5.cloned.1.call-done = f32[128,1,1,1024]{0,3,2,1:T(8,128)} async-done(((f32[512,1,1,1024]{0,3,2,1:T(8,128)}), f32[128,1,1,1024]{0,3,2,1:T(8,128)}) %reduce-scatter.5.cloned.1.call-update) | async-done | bytes 524304 | tf_op jit(solution)/shard_map/reduce_scatter | solution.py:81
  369.7 1.8 convert_element_type.46
  371.5 1.8 copy.130
  373.3 92.4 %all-reduce.6.cloned.1.call-done = bf16[27,128,512]{2,1,0:T(8,128)(2,1)} async-done(((bf16[27,128,512]{2,1,0:T(8,128)(2,1)}), bf16[27,128,512]{2,1,0:T(8,128)(2,1)}) %all-reduce.6.cloned.1.call-update) | async-done | bytes 3538960 | tf_op jit(solution)/shard_map/psum | solution.py:104
  465.6 5.9 %convert_element_type.52 = f32[27,128,512]{2,1,0:T(8,128)} convert(bf16[27,128,512]{2,1,0:T(8,128)(2,1)} %all-reduce.6.cloned.1.call-done) | non-fusion elementwise | flops 1769472 | bytes 10616832 | tf_op jit(solution)/shard_map/convert_element_type | solution.py:104
  (67 shorter events, 4.7 us)
Async XLA Ops:
  7.2 83.2 %copy-start = (bf16[27,128,512]{2,1,0:T(8,128)(2,1)S(1)}, bf16[27,128,512]{2,1,0:T(8,128)(2,1)}, u32[]{:S(2)}) copy-start(bf16[27,128,512]{2,1,0:T(8,128)(2,1)} %param.5) | copy-start | bytes 10616836
  7.2 75.6 %all-gather.3.cloned.1.call-start = ((), (), s32[]{:S(2)}) async-start(), calls=%async_computation.2 | async-start | bytes 3932160 | tf_op jit(solution)/shard_map/all_gather | solution.py:75
  9.2 3.7 collective-permute-start
  11.6 3.6 collective-permute-start.1
  17.2 128.8 %all-gather.5.cloned.1.call-start = ((), (), s32[]{:S(2)}) async-start(), calls=%async_computation.4 | async-start | bytes 3932160 | tf_op jit(solution)/shard_map/all_gather | solution.py:88
  19.0 3.4 collective-permute-start.4
  21.0 3.6 collective-permute-start.5
  26.6 225.8 %all-reduce.4.cloned.1.call-start = ((), (), s32[]{:S(2)}) async-start(), calls=%async_computation.5 | async-start | bytes 7077888 | tf_op jit(solution)/shard_map/psum | solution.py:104
  87.7 22.3 %copy-start.1 = (bf16[512,3,32,1,40]{0,2,4,1,3:T(8,128)(2,1)}, bf16[512,3,32,1,40]{0,2,4,1,3:T(8,128)(2,1)S(1)}, u32[]{:S(2)}) copy-start(bf16[512,3,32,1,40]{0,2,4,1,3:T(8,128)(2,1)S(1)} %get-tuple-element.20) | copy-start | bytes 11796484
  87.8 2.7 copy-start.13
  101.3 0.8 copy-start.6
  102.8 93.5 %collective-permute-start.3 = (bf16[128,1,1,1024]{0,3,2,1:T(8,128)(2,1)}, bf16[128,1,1,1024]{0,3,2,1:T(8,128)(2,1)}, u32[]{:S(2)}, u32[]{:S(2)}) collective-permute-start(bf16[128,1,1,1024]{0,3,2,1:T(8,128)(2,1)} %bitcast.42), channel_id=1, source_target_pairs={{1,0},{3,2},{5,4},{7,6},{9,8},{11,10},{13,12},{15,14},{17,16},{19,... | collective-permute-start | bytes 786440 | tf_op jit(solution)/shard_map/ppermute | solution.py:17
  104.1 93.7 %collective-permute-start.2 = (bf16[128,1,1,1024]{0,3,2,1:T(8,128)(2,1)}, bf16[128,1,1,1024]{0,3,2,1:T(8,128)(2,1)}, u32[]{:S(2)}, u32[]{:S(2)}) collective-permute-start(bf16[128,1,1,1024]{0,3,2,1:T(8,128)(2,1)} %bitcast.42), channel_id=1, source_target_pairs={{0,1},{2,3},{4,5},{6,7},{8,9},{10,11},{12,13},{14,15},{16,17},{18,... | collective-permute-start | bytes 786440 | tf_op jit(solution)/shard_map/ppermute | solution.py:16
  152.4 1.9 copy-start.4
  152.8 3.2 copy-start.3
  156.1 1.8 copy-start.9
  156.1 2.2 copy-start.8
  156.1 2.6 copy-start.2
  158.7 2.7 copy-start.11
  158.7 2.7 copy-start.15
  171.6 1.2 copy-start.10
  194.9 101.0 %all-reduce.8.cloned.1.call-start = ((), (), s32[]{:S(2)}) async-start(), calls=%async_computation.7 | async-start | bytes 7077888 | tf_op jit(solution)/shard_map/psum | solution.py:107
  194.9 4.5 copy-start.7
  202.8 20.1 %copy-start.5 = (bf16[128,1,3,32,32]{0,1,4,3,2:T(2,128)(2,1)}, bf16[128,1,3,32,32]{0,1,4,3,2:T(2,128)(2,1)S(1)}, u32[]{:S(2)}) copy-start(bf16[128,1,3,32,32]{0,1,4,3,2:T(2,128)(2,1)S(1)} %pad_maximum_fusion) | copy-start | bytes 2359300
  222.9 102.5 %reduce-scatter.7.cloned.1.call-start = ((), (), s32[]{:S(2)}) async-start(), calls=%async_computation.8 | async-start | bytes 1310720
  224.0 2.9 collective-permute-start.6
  225.3 3.5 collective-permute-start.7
  226.9 2.8 copy-start.14
  238.9 130.8 %reduce-scatter.5.cloned.1.call-start = ((), (), s32[]{:S(2)}) async-start(), calls=%async_computation.3 | async-start | bytes 2621440 | tf_op jit(solution)/shard_map/reduce_scatter | solution.py:81
  240.9 2.1 copy-start.12
  252.3 213.3 %all-reduce.6.cloned.1.call-start = ((), (), s32[]{:S(2)}) async-start(), calls=%async_computation.6 | async-start | bytes 7077888 | tf_op jit(solution)/shard_map/psum | solution.py:104
Sparse Core Ops, SparseCore 0:
  17.3 65.4 all-gather.2
  84.3 61.5 all-gather.4
  195.0 22.2 all-reduce.3
  223.0 72.8 all-reduce.7
  298.0 27.3 reduce-scatter.6
  327.6 42.1 reduce-scatter.4
  372.9 92.6 all-reduce.5
